TPU v7x, 128 devices: a whole 4x4x4 slice. The times are simulated.
128 devices in a mesh: seq: 32 (over z, y, core), tp: 4 (over x).
Axes of the slice: x: 4, y: 4, z: 4, core: 2. Of those that a mesh axis runs over, the one named last changes fastest.
Arguments:
- states: bfloat16 [256, 3072], P(None, 'seq'), may hold values from -20 to 20
- norm_gain: bfloat16 [3072], P('seq'), may hold values from 0.25 to 1.75
- w_qkv: bfloat16 [3, 3072, 3072], P(None, 'seq', 'tp'), may hold values from -0.109375 to 0.109375
- w_out: bfloat16 [3072, 3072], P('tp', 'seq'), may hold values from -0.109375 to 0.109375
- cache: bfloat16 [768, 2, 64, 3072], P('seq', None, None, 'tp'), may hold values from -400 to 400
- context_len: int32 [256], replicated, may hold values from 1 to 4096, as said below
- block_owner: int32 [768], P('seq'), may hold values from 0 to 256, as said below
- block_index: int32 [768], P('seq'), may hold values from 0 to 63, as said below
Outputs:
- hidden: bfloat16 [256, 3072], P('tp', 'seq')
- updated: bfloat16 [768, 2, 64, 3072], P('seq', None, None, 'tp')
Inputs may be any that keep to these rules, and one draw needn't show every extreme that they name: `context_len`: A request of length n owns exactly ceil(n / 64) pool blocks, with block_index 0, 1, ... once each; at least one pool block is unused. `context_len`: exactly 4 requests own 64/2 blocks or more; every other request owns at most 2 blocks, all on one index of seq. `block_owner`: the value 256 marks an unused block. `block_index`: 0 for an unused block.
All inputs are finite; a program needn't handle non-finite values.
Results may differ from a plain program's by a relative error of at most 0.0068.
Values may be sent and summed in bfloat16 or wider, within the bound.
A program may use at most 128 MiB of HBM per device.

v0:
```python
import jax
import jax.numpy as jnp
from jax import lax
from jax.sharding import PartitionSpec as P

HEAD_DIM = 96
EPSILON = 1e-05
NEG_FLOOR = -1e30


def combined_all(part, axis, combine):
    gathered = jax.tree.map(lambda a: lax.all_gather(a, axis), part)

    def take(source):
        return jax.tree.map(lambda a: lax.dynamic_index_in_dim(a, source, 0, False), gathered)

    return lax.fori_loop(
        1, lax.axis_size(axis), lambda source, state: combine(state, take(source)), take(0)
    )


def rotate(values, positions):
    half_dim = HEAD_DIM // 2
    frequency = 10000.0 ** (-jnp.arange(half_dim, dtype=jnp.float32) * 2.0 / HEAD_DIM)
    angles = positions.astype(jnp.float32)[:, None] * frequency[None, :]
    cosine = jnp.cos(angles)[:, None, :]
    sine_part = jnp.sin(angles)[:, None, :]
    front_half = values[..., :half_dim]
    back_half = values[..., half_dim:]
    return jnp.concatenate(
        [front_half * cosine - back_half * sine_part, back_half * cosine + front_half * sine_part],
        axis=-1,
    )


def finish(projected, positions):
    row_count = projected.shape[0]
    columns = projected.shape[2]
    head_count = columns // HEAD_DIM
    query = rotate(
        projected[:, 0].reshape(row_count, head_count, HEAD_DIM), positions
    ) * HEAD_DIM ** (-0.5)
    keys_new = rotate(projected[:, 1].reshape(row_count, head_count, HEAD_DIM), positions)
    return (
        query.astype(jnp.bfloat16).reshape(row_count, columns),
        keys_new.astype(jnp.bfloat16).reshape(row_count, columns),
        projected[:, 2].astype(jnp.bfloat16),
    )


def join(earlier, later):
    highest = jnp.maximum(earlier[0], later[0])
    left_scale = jnp.exp(earlier[0] - highest)
    right_scale = jnp.exp(later[0] - highest)
    return (
        highest,
        earlier[1] * left_scale + later[1] * right_scale,
        earlier[2] * jnp.repeat(left_scale, HEAD_DIM, axis=1)
        + later[2] * jnp.repeat(right_scale, HEAD_DIM, axis=1),
    )


def shards(states, norm_gain, w_qkv, w_out, cache, context_len, block_owner, block_index):
    requests = states.shape[0]
    seq_count = lax.axis_size("seq")
    wide_states = states.astype(jnp.float32)
    sum_squares = lax.psum(jnp.sum(wide_states * wide_states, axis=1), "seq")
    inverse = lax.rsqrt(sum_squares / (states.shape[1] * seq_count) + EPSILON)
    normed = (wide_states * inverse[:, None] * norm_gain.astype(jnp.float32)[None, :]).astype(
        jnp.bfloat16
    )
    positions = context_len - 1
    local_term = jnp.einsum("rd,cdh->rch", normed, w_qkv, preferred_element_type=jnp.float32)
    projected = lax.psum(local_term, "seq")
    query, keys_new, values_new = finish(projected, positions)
    blocks, _, tokens, columns = cache.shape
    head_count = columns // HEAD_DIM
    block_live = block_owner < requests
    owner_row = jnp.minimum(block_owner, requests - 1)
    last_position = positions[owner_row]
    block_hit = block_live & (block_index == last_position // tokens)
    slot_hit = block_hit[:, None] & (
        jnp.arange(tokens, dtype=jnp.int32)[None, :] == (last_position % tokens)[:, None]
    )
    fresh_rows = jnp.stack([keys_new[owner_row], values_new[owner_row]], axis=1)
    updated = jnp.where(slot_hit[:, None, :, None], fresh_rows[:, :, None, :], cache)
    query_rows = query[owner_row].reshape(blocks, head_count, HEAD_DIM)
    key_cache = updated[:, 0].reshape(blocks, tokens, head_count, HEAD_DIM)
    value_cache = updated[:, 1].reshape(blocks, tokens, head_count, HEAD_DIM)
    scores = jnp.einsum("bhd,bthd->bht", query_rows, key_cache, preferred_element_type=jnp.float32)
    token_position = block_index[:, None] * tokens + jnp.arange(tokens, dtype=jnp.int32)[None, :]
    visible = block_live[:, None] & (token_position < context_len[owner_row][:, None])
    masked = jnp.where(visible[:, None, :], scores, NEG_FLOOR)
    block_max = jnp.max(masked, axis=-1)
    weights = jnp.where(visible[:, None, :], jnp.exp(masked - block_max[..., None]), 0.0).astype(
        jnp.bfloat16
    )
    block_sum = jnp.sum(weights.astype(jnp.float32), axis=-1)
    block_out = jnp.einsum(
        "bht,bthd->bhd", weights, value_cache, preferred_element_type=jnp.float32
    ).reshape(blocks, columns)
    segment = jnp.where(block_live, block_owner, requests)
    member = segment[None, :] == jnp.arange(requests, dtype=jnp.int32)[:, None]
    local_max = jnp.max(jnp.where(member[:, :, None], block_max[None, :, :], NEG_FLOOR), axis=1)
    factor = jnp.exp(block_max - local_max[owner_row])
    member_matrix = member.astype(jnp.float32)
    totals = jnp.dot(member_matrix, block_sum * factor, precision=lax.Precision.HIGHEST)
    outputs = jnp.dot(
        member_matrix,
        block_out * jnp.repeat(factor, HEAD_DIM, axis=1),
        precision=lax.Precision.HIGHEST,
    )
    merged = combined_all((local_max, totals, outputs), "seq", join)
    attended = (merged[2] / jnp.repeat(merged[1], HEAD_DIM, axis=1)).astype(jnp.bfloat16)
    terms = jnp.dot(attended, w_out, preferred_element_type=jnp.float32)
    summed = lax.psum_scatter(terms, "tp", scatter_dimension=0, tiled=True)
    row_count = summed.shape[0]
    residual_rows = lax.dynamic_slice_in_dim(
        wide_states, lax.axis_index("tp") * row_count, row_count, 0
    )
    hidden = (summed + residual_rows).astype(jnp.bfloat16)
    return (hidden, updated)


def solution(mesh):
    return jax.shard_map(
        shards,
        mesh=mesh,
        in_specs=(
            P(None, "seq"),
            P("seq"),
            P(None, "seq", "tp"),
            P("tp", "seq"),
            P("seq", None, None, "tp"),
            P(),
            P("seq"),
            P("seq"),
        ),
        out_specs=(P("tp", "seq"), P("seq", None, None, "tp")),
        check_vma=False,
    )
```

profile of v0, /device:TPU:0, one launch (start us, length us, event | category | flops | bytes accessed | tf_op | source)
XLA Modules:
  0.0 399.5 jit_solution(8305740966183515385)
XLA Ops:
  7.2 0.9 multiply_reduce_fusion
  8.1 68.7 %psum.14 = f32[256]{0:T(256)S(1)} all-reduce(f32[256]{0:T(256)S(1)} %multiply_reduce_fusion), channel_id=1, replica_groups=mesh['seq'=32,'tp'=4] {'seq'}, use_global_device_ids=true, to_apply=%region_1.0 | all-reduce | flops 256 | bytes 2048 | tf_op jit(solution)/shard_map/psum | solution.py:67
  76.8 0.7 convert_element_type.43
  77.5 2.8 fusion.12
  80.4 0.7 gather_fusion
  81.1 0.7 gather_fusion.2
  82.3 102.0 %all-reduce.2.cloned.1.call-done = f32[256,3,768]{2,0,1:T(8,128)} async-done(((f32[256,3,768]{2,0,1:T(8,128)}), f32[256,3,768]{2,0,1:T(8,128)}) %all-reduce.2.cloned.1.call-update) | async-done | bytes 2359312 | tf_op jit(solution)/shard_map/psum | solution.py:74
  184.3 1.5 fusion.28
  186.3 1.1 subtract_convert_fusion
  187.6 0.6 gather_fusion.3
  188.2 1.2 fusion.9
  189.4 0.6 gather_fusion.4
  190.1 2.7 broadcast_select_fusion
  192.8 2.2 fusion.27
  195.0 0.7 copy-done.2
  195.7 6.4 %reshape_squeeze.14 = bf16[24,64,8,96]{3,2,1,0:T(8,128)(2,1)} reshape(bf16[24,1,64,768]{3,2,1,0:T(8,128)(2,1)} %get-tuple-element.239) | data formatting | bytes 4718592 | tf_op jit(solution)/shard_map/reshape;squeeze | solution.py:88
  202.2 1.2 fusion.7
  203.3 0.9 copy.50
  204.3 1.7 gather_fusion.1
  206.1 3.6 fusion.5
  210.0 4.3 %reshape_squeeze.15 = bf16[24,64,8,96]{3,2,1,0:T(8,128)(2,1)} reshape(bf16[24,1,64,768]{3,2,1,0:T(8,128)(2,1)S(1)} %get-tuple-element.238) | data formatting | bytes 4718592 | tf_op jit(solution)/shard_map/reshape;squeeze | solution.py:89
  214.5 0.6 gather_fusion.5
  215.1 2.8 fusion.3
  218.1 1.5 fusion.17
  219.9 25.3 %all-gather.1 = f32[8192,8]{0,1:T(8,128)S(1)} all-gather(f32[256,8]{0,1:T(8,128)S(1)} %fusion.18), channel_id=3, replica_groups=mesh['seq'=32,'tp'=4] {'seq'}, dimensions={0}, use_global_device_ids=true | all-gather | bytes 270336 | tf_op jit(solution)/shard_map/all_gather | solution.py:12
  245.2 22.3 %all-gather = f32[8192,8]{0,1:T(8,128)S(1)} all-gather(f32[256,8]{0,1:T(8,128)S(1)} %select_reduce_fusion), channel_id=2, replica_groups=mesh['seq'=32,'tp'=4] {'seq'}, dimensions={0}, use_global_device_ids=true | all-gather | bytes 270336 | tf_op jit(solution)/shard_map/all_gather | solution.py:12
  267.5 44.9 %all-gather.5.cloned.1.call-done = f32[8192,768]{1,0:T(8,128)} async-done(((f32[256,768]{1,0:T(8,128)}), f32[8192,768]{1,0:T(8,128)}) %all-gather.5.cloned.1.call-update) | async-done | bytes 25165840 | tf_op jit(solution)/shard_map/all_gather | solution.py:12
  312.5 1.2 slice.66
  313.9 56.6 %while.19 = (s32[]{:T(128)}, f32[256,8]{0,1:T(8,128)S(1)}, f32[256,8]{0,1:T(8,128)S(1)}, f32[256,768]{0,1:T(8,128)S(1)}, f32[32,256,8]{1,2,0:T(8,128)S(1)}, /*in...) while((s32[]{:T(128)}, f32[256,8]{0,1:T(8,128)S(1)}, ...), condition=%wide.region_7.8_spmd, body=%wide.region_6.7_spmd.sunk | while | flops 602117 | bytes 5587095 | solution.py:17
  314.0 1.2 constant_dynamic-slice_fusion.2
  315.8 1.2 constant_dynamic-slice_fusion.2
  317.7 1.2 constant_dynamic-slice_fusion.2
  319.5 1.2 constant_dynamic-slice_fusion.2
  321.3 1.2 constant_dynamic-slice_fusion.2
  323.1 1.2 constant_dynamic-slice_fusion.2
  325.0 1.2 constant_dynamic-slice_fusion.2
  326.8 1.2 constant_dynamic-slice_fusion.2
  328.6 1.2 constant_dynamic-slice_fusion.2
  330.4 1.2 constant_dynamic-slice_fusion.2
  332.2 1.2 constant_dynamic-slice_fusion.2
  334.1 1.2 constant_dynamic-slice_fusion.2
  335.9 1.2 constant_dynamic-slice_fusion.2
  337.7 1.2 constant_dynamic-slice_fusion.2
  339.5 1.2 constant_dynamic-slice_fusion.2
  341.4 1.2 constant_dynamic-slice_fusion.2
  343.2 1.2 constant_dynamic-slice_fusion.2
  345.0 1.2 constant_dynamic-slice_fusion.2
  346.8 1.2 constant_dynamic-slice_fusion.2
  348.7 1.2 constant_dynamic-slice_fusion.2
  350.5 1.2 constant_dynamic-slice_fusion.2
  352.3 1.2 constant_dynamic-slice_fusion.2
  354.1 1.2 constant_dynamic-slice_fusion.2
  356.0 1.2 constant_dynamic-slice_fusion.2
  357.8 1.2 constant_dynamic-slice_fusion.2
  359.6 1.2 constant_dynamic-slice_fusion.2
  361.4 1.2 constant_dynamic-slice_fusion.2
  363.3 1.2 constant_dynamic-slice_fusion.2
  365.1 1.2 constant_dynamic-slice_fusion.2
  366.9 1.2 constant_dynamic-slice_fusion.2
  368.7 1.2 constant_dynamic-slice_fusion.2
  370.6 1.0 fusion.29
  371.6 19.7 %reduce-scatter.4.cloned.1.call-done = f32[64,96]{1,0:T(8,128)} async-done(((f32[256,96]{1,0:T(8,128)}), f32[64,96]{1,0:T(8,128)}) %reduce-scatter.4.cloned.1.call-update) | async-done | bytes 24592
  391.3 0.8 copy.67
  392.3 0.7 copy.58
  (144 shorter events, 21.4 us)
Async XLA Ops:
  7.2 70.3 %copy-start = (bf16[3,96,768]{2,1,0:T(8,128)(2,1)S(1)}, bf16[3,96,768]{2,1,0:T(8,128)(2,1)}, u32[]{:S(2)}) copy-start(bf16[3,96,768]{2,1,0:T(8,128)(2,1)} %param.12) | copy-start | bytes 1327108
  7.2 73.1 %copy-start.1 = (s32[256]{0:T(256)S(1)}, s32[256]{0:T(256)}, u32[]{:S(2)}) copy-start(s32[256]{0:T(256)} %param.15) | copy-start | bytes 3076
  7.2 73.1 %copy-start.5 = (s32[24]{0:T(128)S(1)}, s32[24]{0:T(128)}, u32[]{:S(2)}) copy-start(s32[24]{0:T(128)} %param.16) | copy-start | bytes 292
  7.2 177.1 %all-reduce.2.cloned.1.call-start = ((), (), s32[]{:S(2)}) async-start(), calls=%async_computation.1 | async-start | bytes 4718592 | tf_op jit(solution)/shard_map/psum | solution.py:74
  8.1 73.7 %copy-start.6 = (s32[24]{0:T(128)S(1)}, s32[24]{0:T(128)}, u32[]{:S(2)}) copy-start(s32[24]{0:T(128)} %param.17) | copy-start | bytes 292
  80.3 232.2 %all-gather.5.cloned.1.call-start = ((), (), s32[]{:S(2)}) async-start(), calls=%async_computation.2 | async-start | bytes 25952256 | tf_op jit(solution)/shard_map/all_gather | solution.py:12
  192.8 2.9 copy-start.2
  219.7 171.6 %reduce-scatter.4.cloned.1.call-start = ((), (), s32[]{:S(2)}) async-start(), calls=%async_computation.3 | async-start | bytes 163840
  313.9 56.7 %copy-start.4 = (bf16[768,96]{0,1:T(8,128)(2,1)S(1)}, bf16[768,96]{0,1:T(8,128)(2,1)}, u32[]{:S(2)}) copy-start(bf16[768,96]{0,1:T(8,128)(2,1)} %param.13) | copy-start | bytes 442372
  313.9 57.7 %copy-start.3 = (bf16[256,96]{0,1:T(8,128)(2,1)S(1)}, bf16[256,96]{0,1:T(8,128)(2,1)}, u32[]{:S(2)}) copy-start(bf16[256,96]{0,1:T(8,128)(2,1)} %param.10) | copy-start | bytes 147460
Sparse Core Ops, SparseCore 0:
  80.4 103.8 all-reduce.1
  219.8 92.5 all-gather.4
  371.7 19.5 reduce-scatter.3
where the time goes:
time: 402 us; the launch traced here: 399 us
  waiting for transfers between devices  167 us (42%)
  blocking collectives  116 us (29%)
  local copies, waits for them, and re-layouts  71.3 us (18%)
  other arithmetic  18 us (4%)
  between operations  14.1 us (4%)
  matrix products  11.8 us (3%)
    psum x1, waiting for transfers between devices, shards(): projected = lax.psum(local_term, 'seq')  102 us
    psum x1, blocking collectives, shards(): sum_squares = lax.psum(jnp.sum(wide_states * wide_states, axis=1), 'seq')  68.7 us
    all_gather x2, blocking collectives, combined_all(): gathered = jax.tree.map(lambda a: lax.all_gather(a, axis), part)  47.6 us
    dynamic_slice x65, local copies, waits for them, and re-layouts, take(): lax.dynamic_index_in_dim(a, source, 0, False)  46.3 us
    all_gather x1, waiting for transfers between devices, combined_all(): gathered = jax.tree.map(lambda a: lax.all_gather(a, axis), part)  44.9 us
    unnamed x4, waiting for transfers between devices  19.8 us
    add x31, other arithmetic, join(): earlier[2] * jnp.repeat(left_scale, HEAD_DIM, axis=1)  9.66 us
  transfers between devices with their start and end apart: 3, of which 3 were waited for; matrix products, arithmetic and copies ran while one was open for 1% of the time, Pallas kernels for 0%

commit v1 on v0

--- a/solution.py
+++ b/solution.py
@@ -71,7 +71,13 @@
     )
     positions = context_len - 1
     local_term = jnp.einsum("rd,cdh->rch", normed, w_qkv, preferred_element_type=jnp.float32)
-    projected = lax.psum(local_term, "seq")
+    num = lax.axis_size("seq")
+    projected, w2 = (local_term, 0)
+    while 1 << w2 < num:
+        current_arr = tuple(((dev, dev ^ 1 << w2) for dev in range(num)))
+        y2 = lax.ppermute(projected, "seq", current_arr)
+        projected = projected + y2
+        w2 = w2 + 1
     query, keys_new, values_new = finish(projected, positions)
     blocks, _, tokens, columns = cache.shape
     head_count = columns // HEAD_DIM

time: 402 us -> 509 us (1.27)
  waiting for transfers between devices: 167 us -> 276 us
    ppermute x0 -> x5, waiting for transfers between devices: none -> 214 us  [shards(): y2 = lax.ppermute(projected, 'seq', current_arr)]
    psum x1 -> x0, waiting for transfers between devices: 102 us -> none  [shards(): projected = lax.psum(local_term, 'seq')]
    unnamed x4 -> x3, waiting for transfers between devices: 19.8 us -> 19.8 us
  transfers between devices with their start and end apart: 3 -> 7, of which waited for: 3 -> 7; matrix products, arithmetic and copies ran while one was open for 1% -> 0% of each run, Pallas kernels for 0% -> 0%
where the time goes in v1:
time: 509 us; the launch traced here: 507 us
  waiting for transfers between devices  276 us (54%)
  blocking collectives  116 us (23%)
  local copies, waits for them, and re-layouts  67.8 us (13%)
  other arithmetic  20.8 us (4%)
  between operations  14.5 us (3%)
  matrix products  10.5 us (2%)
    ppermute x5, waiting for transfers between devices, shards(): y2 = lax.ppermute(projected, 'seq', current_arr)  214 us
    psum x1, blocking collectives, shards(): sum_squares = lax.psum(jnp.sum(wide_states * wide_states, axis=1), 'seq')  68.7 us
    all_gather x2, blocking collectives, combined_all(): gathered = jax.tree.map(lambda a: lax.all_gather(a, axis), part)  46.9 us
    dynamic_slice x65, local copies, waits for them, and re-layouts, take(): lax.dynamic_index_in_dim(a, source, 0, False)  46.3 us
    all_gather x1, waiting for transfers between devices, combined_all(): gathered = jax.tree.map(lambda a: lax.all_gather(a, axis), part)  43.1 us
    unnamed x3, waiting for transfers between devices  19.8 us
  transfers between devices with their start and end apart: 7, of which 7 were waited for; matrix products, arithmetic and copies ran while one was open for 0% of the time, Pallas kernels for 0%

profile of v1, /device:TPU:0, one launch (start us, length us, event | category | flops | bytes accessed | tf_op | source)
XLA Modules:
  0.0 507.2 jit_solution(3845944303299470930)
XLA Ops:
  7.2 0.9 multiply_reduce_fusion
  8.1 68.7 %psum.7 = f32[256]{0:T(256)S(1)} all-reduce(f32[256]{0:T(256)S(1)} %multiply_reduce_fusion), channel_id=1, replica_groups=mesh['seq'=32,'tp'=4] {'seq'}, use_global_device_ids=true, to_apply=%region_1.0 | all-reduce | flops 256 | bytes 2048 | tf_op jit(solution)/shard_map/psum | solution.py:67
  76.8 0.7 convert_element_type.43
  77.4 1.4 fusion.12
  78.9 4.5 collective-permute-done
  83.8 53.3 %collective-permute-done.1 = f32[256,3,768]{2,0,1:T(8,128)S(1)} collective-permute-done((f32[256,3,768]{2,0,1:T(8,128)S(1)}, f32[256,3,768]{2,0,1:T(8,128)S(1)}, u32[]{:S(2)}, u32[]{:S(2)}) %collective-permute-start.1) | collective-permute-done | bytes 2359328 | tf_op jit(solution)/shard_map/ppermute | solution.py:78
  137.5 54.0 %collective-permute-done.2 = f32[256,3,768]{2,0,1:T(8,128)S(1)} collective-permute-done((f32[256,3,768]{2,0,1:T(8,128)S(1)}, f32[256,3,768]{2,0,1:T(8,128)S(1)}, u32[]{:S(2)}, u32[]{:S(2)}) %collective-permute-start.2) | collective-permute-done | bytes 2359328 | tf_op jit(solution)/shard_map/ppermute | solution.py:78
  191.8 52.2 %collective-permute-done.3 = f32[256,3,768]{2,0,1:T(8,128)S(1)} collective-permute-done((f32[256,3,768]{2,0,1:T(8,128)S(1)}, f32[256,3,768]{2,0,1:T(8,128)S(1)}, u32[]{:S(2)}, u32[]{:S(2)}) %collective-permute-start.3) | collective-permute-done | bytes 2359328 | tf_op jit(solution)/shard_map/ppermute | solution.py:78
  244.5 0.7 gather_fusion
  245.2 0.7 gather_fusion.2
  246.4 49.6 %collective-permute-done.4 = f32[256,3,768]{2,0,1:T(8,128)} collective-permute-done((f32[256,3,768]{2,0,1:T(8,128)S(1)}, f32[256,3,768]{2,0,1:T(8,128)}, u32[]{:S(2)}, u32[]{:S(2)}) %collective-permute-start.4) | collective-permute-done | bytes 2359328 | tf_op jit(solution)/shard_map/ppermute | solution.py:78
  296.0 2.0 add.146
  298.0 0.8 fusion.9
  299.4 1.0 subtract_convert_fusion
  300.5 0.6 gather_fusion.3
  301.8 2.7 broadcast_select_fusion
  304.6 2.2 fusion.27
  306.8 0.7 copy-done.3
  307.5 6.4 %reshape_squeeze.14 = bf16[24,64,8,96]{3,2,1,0:T(8,128)(2,1)} reshape(bf16[24,1,64,768]{3,2,1,0:T(8,128)(2,1)} %get-tuple-element.239) | data formatting | bytes 4718592 | tf_op jit(solution)/shard_map/reshape;squeeze | solution.py:94
  313.9 1.1 fusion.7
  315.9 3.6 fusion.5
  319.8 4.4 reshape_squeeze.15
  325.0 2.8 fusion.3
  328.0 1.6 fusion.17
  329.8 23.3 %all-gather.1 = f32[8192,8]{0,1:T(8,128)S(1)} all-gather(f32[256,8]{0,1:T(8,128)S(1)} %fusion.18), channel_id=3, replica_groups=mesh['seq'=32,'tp'=4] {'seq'}, dimensions={0}, use_global_device_ids=true | all-gather | bytes 270336 | tf_op jit(solution)/shard_map/all_gather | solution.py:12
  353.1 23.6 %all-gather = f32[8192,8]{0,1:T(8,128)S(1)} all-gather(f32[256,8]{0,1:T(8,128)S(1)} %select_reduce_fusion), channel_id=2, replica_groups=mesh['seq'=32,'tp'=4] {'seq'}, dimensions={0}, use_global_device_ids=true | all-gather | bytes 270336 | tf_op jit(solution)/shard_map/all_gather | solution.py:12
  376.7 43.1 %all-gather.5.cloned.1.call-done = f32[8192,768]{1,0:T(8,128)} async-done(((f32[256,768]{1,0:T(8,128)}), f32[8192,768]{1,0:T(8,128)}) %all-gather.5.cloned.1.call-update) | async-done | bytes 25165840 | tf_op jit(solution)/shard_map/all_gather | solution.py:12
  419.8 1.2 slice.66
  421.3 56.6 %while.19 = (s32[]{:T(128)}, f32[256,8]{0,1:T(8,128)S(1)}, f32[256,8]{0,1:T(8,128)S(1)}, f32[256,768]{0,1:T(8,128)S(1)}, f32[32,256,8]{1,2,0:T(8,128)S(1)}, /*in...) while((s32[]{:T(128)}, f32[256,8]{0,1:T(8,128)S(1)}, ...), condition=%wide.region_6.7_spmd, body=%wide.region_5.6_spmd.sunk | while | flops 602117 | bytes 5587095 | solution.py:17
  421.3 1.2 constant_dynamic-slice_fusion.2
  423.2 1.2 constant_dynamic-slice_fusion.2
  425.0 1.2 constant_dynamic-slice_fusion.2
  426.8 1.2 constant_dynamic-slice_fusion.2
  428.6 1.2 constant_dynamic-slice_fusion.2
  430.5 1.2 constant_dynamic-slice_fusion.2
  432.3 1.2 constant_dynamic-slice_fusion.2
  434.1 1.2 constant_dynamic-slice_fusion.2
  435.9 1.2 constant_dynamic-slice_fusion.2
  437.7 1.2 constant_dynamic-slice_fusion.2
  439.6 1.2 constant_dynamic-slice_fusion.2
  441.4 1.2 constant_dynamic-slice_fusion.2
  443.2 1.2 constant_dynamic-slice_fusion.2
  445.0 1.2 constant_dynamic-slice_fusion.2
  446.9 1.2 constant_dynamic-slice_fusion.2
  448.7 1.2 constant_dynamic-slice_fusion.2
  450.5 1.2 constant_dynamic-slice_fusion.2
  452.3 1.2 constant_dynamic-slice_fusion.2
  454.2 1.2 constant_dynamic-slice_fusion.2
  456.0 1.2 constant_dynamic-slice_fusion.2
  457.8 1.2 constant_dynamic-slice_fusion.2
  459.6 1.2 constant_dynamic-slice_fusion.2
  461.5 1.2 constant_dynamic-slice_fusion.2
  463.3 1.2 constant_dynamic-slice_fusion.2
  465.1 1.2 constant_dynamic-slice_fusion.2
  466.9 1.2 constant_dynamic-slice_fusion.2
  468.8 1.2 constant_dynamic-slice_fusion.2
  470.6 1.2 constant_dynamic-slice_fusion.2
  472.4 1.2 constant_dynamic-slice_fusion.2
  474.2 1.2 constant_dynamic-slice_fusion.2
  476.1 1.2 constant_dynamic-slice_fusion.2
  477.9 1.0 fusion.29
  479.0 19.8 %reduce-scatter.4.cloned.1.call-done = f32[64,96]{1,0:T(8,128)} async-done(((f32[256,96]{1,0:T(8,128)}), f32[64,96]{1,0:T(8,128)}) %reduce-scatter.4.cloned.1.call-update) | async-done | bytes 24592
  498.7 0.8 copy.67
  499.7 0.7 copy.58
  (160 shorter events, 24.9 us)
Async XLA Ops:
  7.2 70.3 %copy-start = (bf16[3,96,768]{2,1,0:T(8,128)(2,1)S(1)}, bf16[3,96,768]{2,1,0:T(8,128)(2,1)}, u32[]{:S(2)}) copy-start(bf16[3,96,768]{2,1,0:T(8,128)(2,1)} %param.12) | copy-start | bytes 1327108
  7.2 412.6 %all-gather.5.cloned.1.call-start = ((), (), s32[]{:S(2)}) async-start(), calls=%async_computation.1 | async-start | bytes 25952256 | tf_op jit(solution)/shard_map/all_gather | solution.py:12
  78.8 4.6 collective-permute-start
  83.7 53.4 %collective-permute-start.1 = (f32[256,3,768]{2,0,1:T(8,128)S(1)}, f32[256,3,768]{2,0,1:T(8,128)S(1)}, u32[]{:S(2)}, u32[]{:S(2)}) collective-permute-start(f32[256,3,768]{2,0,1:T(8,128)S(1)} %add.142), channel_id=1, source_target_pairs={{0,8},{4,12},{8,0},{12,4},{16,24},{20,28},{24,16},{28,20},{32,40},... | collective-permute-start | bytes 7077896 | tf_op jit(solution)/shard_map/ppermute | solution.py:78
  137.4 54.0 %collective-permute-start.2 = (f32[256,3,768]{2,0,1:T(8,128)S(1)}, f32[256,3,768]{2,0,1:T(8,128)S(1)}, u32[]{:S(2)}, u32[]{:S(2)}) collective-permute-start(f32[256,3,768]{2,0,1:T(8,128)S(1)} %add.143), channel_id=1, source_target_pairs={{0,16},{4,20},{8,24},{12,28},{16,0},{20,4},{24,8},{28,12},{32,48},... | collective-permute-start | bytes 7077896 | tf_op jit(solution)/shard_map/ppermute | solution.py:78
  191.7 52.7 %copy-start.7 = (s32[24]{0:T(128)S(1)}, s32[24]{0:T(128)}, u32[]{:S(2)}) copy-start(s32[24]{0:T(128)} %param.16) | copy-start | bytes 292
  191.7 52.7 %copy-start.2 = (s32[256]{0:T(256)S(1)}, s32[256]{0:T(256)}, u32[]{:S(2)}) copy-start(s32[256]{0:T(256)} %param.15) | copy-start | bytes 3076
  191.7 54.2 %copy-start.8 = (s32[24]{0:T(128)S(1)}, s32[24]{0:T(128)}, u32[]{:S(2)}) copy-start(s32[24]{0:T(128)} %param.17) | copy-start | bytes 292
  191.7 52.3 %collective-permute-start.3 = (f32[256,3,768]{2,0,1:T(8,128)S(1)}, f32[256,3,768]{2,0,1:T(8,128)S(1)}, u32[]{:S(2)}, u32[]{:S(2)}) collective-permute-start(f32[256,3,768]{2,0,1:T(8,128)S(1)} %add.144), channel_id=1, source_target_pairs={{0,32},{4,36},{8,40},{12,44},{16,48},{20,52},{24,56},{28,60},{32,0... | collective-permute-start | bytes 7077896 | tf_op jit(solution)/shard_map/ppermute | solution.py:78
  244.3 51.6 %collective-permute-start.4 = (f32[256,3,768]{2,0,1:T(8,128)S(1)}, f32[256,3,768]{2,0,1:T(8,128)}, u32[]{:S(2)}, u32[]{:S(2)}) collective-permute-start(f32[256,3,768]{2,0,1:T(8,128)S(1)} %add.145), channel_id=1, source_target_pairs={{0,64},{4,68},{8,72},{12,76},{16,80},{20,84},{24,88},{28,92},{32,9... | collective-permute-start | bytes 7077896 | tf_op jit(solution)/shard_map/ppermute | solution.py:78
  299.4 1.8 copy-start.4
  304.6 2.9 copy-start.3
  329.6 169.2 %reduce-scatter.4.cloned.1.call-start = ((), (), s32[]{:S(2)}) async-start(), calls=%async_computation.2 | async-start | bytes 163840
  421.2 56.7 %copy-start.6 = (bf16[768,96]{0,1:T(8,128)(2,1)S(1)}, bf16[768,96]{0,1:T(8,128)(2,1)}, u32[]{:S(2)}) copy-start(bf16[768,96]{0,1:T(8,128)(2,1)} %param.13) | copy-start | bytes 442372
  421.3 57.7 %copy-start.5 = (bf16[256,96]{0,1:T(8,128)(2,1)S(1)}, bf16[256,96]{0,1:T(8,128)(2,1)}, u32[]{:S(2)}) copy-start(bf16[256,96]{0,1:T(8,128)(2,1)} %param.10) | copy-start | bytes 147460
  477.8 22.5 %copy-start.1 = (bf16[3,96,768]{2,1,0:T(8,128)(2,1)S(1)}, bf16[3,96,768]{2,1,0:T(8,128)(2,1)}, u32[]{:S(2)}) copy-start(bf16[3,96,768]{2,1,0:T(8,128)(2,1)} %param.12) | copy-start | bytes 1327108
Sparse Core Ops, SparseCore 0:
  329.7 90.0 all-gather.4
  479.0 19.6 reduce-scatter.3
